TPU v7x, 256 devices: a whole 4x4x8 slice. The times are simulated.
256 devices in a mesh: grp: 4 (over x_lo, core), row: 4 (over y), col: 16 (over z, x_hi).
Axes of the slice: x: 4 (x_hi: 2, x_lo: 2; x = x_hi * 2 + x_lo), y: 4, z: 8, core: 2. Of those that a mesh axis runs over, the one named last changes fastest.
Arguments:
- block_rows: bfloat16 [8, 304, 10240], P('grp', None, ('row', 'col')), may hold values from -6 to 6
- inverse_factor: float32 [8, 304, 304], P('grp'), as said below
- live_rows: int32 [8], P('grp'), may hold values from 50 to 304, as said below
- shift: float32 [10240], P(('grp', 'row', 'col')), may hold values from 0.5 to 2
Outputs:
- factored: float32 [10240, 10240], P(('grp', 'row'), 'col')
Inputs may be any that keep to these rules, and one draw needn't show every extreme that they name: `live_rows`: every block uses between 50 and 304 rows; some block uses exactly 304 and some exactly 50. `inverse_factor`: each block's matrix is lower triangular with a positive diagonal.
All inputs are finite; a program needn't handle non-finite values.
Results may differ from a plain program's by a relative error of at most 0.0043.
Values may be sent and summed in bfloat16 or wider, within the bound.
A program may use at most 128 MiB of HBM per device.

v0:
```python
import functools

import jax
import jax.numpy as jnp
from jax import lax
from jax.experimental import pallas as pl
from jax.experimental.pallas import tpu as pltpu
from jax.sharding import PartitionSpec as P

PW = 1024
PANELS = 1
NPAN = 10
HI = lax.Precision.HIGHEST
MESH = pl.DeviceIdType.MESH


def _gather_kernel(x_ref, out_ref, local_sem, send_sem, recv_sem, *, axis, count):
    me = lax.axis_index(axis)
    barrier = pltpu.get_barrier_semaphore()
    for step in range(1, count):
        peer = lax.rem(me + step, count)
        pl.semaphore_signal(barrier, inc=1, device_id={axis: peer}, device_id_type=MESH)
    pl.semaphore_wait(barrier, count - 1)
    own = pltpu.make_async_copy(x_ref, out_ref.at[me], local_sem)
    own.start()
    copies = []
    for step in range(1, count):
        peer = lax.rem(me + step, count)
        copy = pltpu.make_async_remote_copy(
            src_ref=x_ref,
            dst_ref=out_ref.at[me],
            send_sem=send_sem.at[step],
            recv_sem=recv_sem.at[step],
            device_id={axis: peer},
            device_id_type=MESH,
        )
        copy.start()
        copies.append(copy)
    own.wait()
    for copy in copies:
        copy.wait()


def remote_gather(x, axis, count, collective_id):
    return pl.pallas_call(
        functools.partial(_gather_kernel, axis=axis, count=count),
        out_shape=jax.ShapeDtypeStruct((count,) + x.shape, x.dtype),
        in_specs=[pl.BlockSpec(memory_space=pl.ANY)],
        out_specs=pl.BlockSpec(memory_space=pl.ANY),
        scratch_shapes=[
            pltpu.SemaphoreType.DMA(()),
            pltpu.SemaphoreType.DMA((count,)),
            pltpu.SemaphoreType.DMA((count,)),
        ],
        compiler_params=pltpu.CompilerParams(collective_id=collective_id, has_side_effects=True),
    )(x)


def _base_inverse(s):
    b = s.shape[0]
    lane = lax.broadcasted_iota(jnp.int32, (b, b), 1)
    sub = lax.broadcasted_iota(jnp.int32, (b, b), 0)
    sub_col = lax.broadcasted_iota(jnp.int32, (b, 1), 0)
    lane_row = lax.broadcasted_iota(jnp.int32, (1, b), 1)
    eye = jnp.where(lane == sub, 1.0, 0.0).astype(jnp.float32)

    width = 4

    def step(i, carry):
        work, inv = carry
        first = width * i
        rows = [jnp.sum(jnp.where(sub == first + q, work, 0.0), axis=0, keepdims=True)
                for q in range(width)]
        cols = [jnp.sum(jnp.where(lane == first + q, work, 0.0), axis=1, keepdims=True)
                for q in range(width)]
        invs = [jnp.sum(jnp.where(sub == first + q, inv, 0.0), axis=0, keepdims=True)
                for q in range(width)]
        block = [[jnp.sum(jnp.where(lane_row == first + r, rows[q], 0.0), axis=1, keepdims=True)
                  for r in range(width)] for q in range(width)]
        small = [[None] * width for _ in range(width)]
        scales = []
        for q in range(width):
            for p in range(q):
                acc = block[p][q]
                for t in range(p):
                    acc = acc - small[q][t] * small[p][t]
                small[q][p] = acc * scales[p]
            d = block[q][q]
            for t in range(q):
                d = d - small[q][t] * small[q][t]
            scales.append(lax.rsqrt(d))
        lcols, lrows, xrows = [], [], []
        for q in range(width):
            c, r, x = cols[q], rows[q], invs[q]
            for p in range(q):
                c = c - lcols[p] * small[q][p]
                r = r - lrows[p] * small[q][p]
                x = x - (small[q][p] * scales[p]) * xrows[p]
            lcols.append(jnp.where(sub_col >= first + q, c * scales[q], 0.0))
            lrows.append(jnp.where(lane_row >= first + q, r * scales[q], 0.0))
            xrows.append(x)
        for q in range(width):
            work = work - lcols[q] * lrows[q]
            u = jnp.where(sub_col == first + q, lcols[q] - 1.0, lcols[q]) * scales[q]
            inv = inv - u * xrows[q]
        return work, inv

    _, inv = lax.fori_loop(0, b // width, step, (s, eye))
    return inv


def _kernel(a_ref, z_ref, *, n, b):
    z_ref[...] = jnp.zeros_like(z_ref)
    for k in range(n // b):
        lo = k * b
        s = a_ref[lo:lo + b, lo:lo + b]
        if k > 0:
            zk = z_ref[0:lo, 0:lo]
            left = lax.dot_general(a_ref[lo:lo + b, 0:lo], zk, (((1,), (1,)), ((), ())),
                                   precision=HI, preferred_element_type=jnp.float32)
            s = s - lax.dot_general(left, left, (((1,), (1,)), ((), ())),
                                    precision=HI, preferred_element_type=jnp.float32)
        d = _base_inverse(s)
        z_ref[lo:lo + b, lo:lo + b] = d
        if k > 0:
            t = jnp.dot(left, zk, precision=HI, preferred_element_type=jnp.float32)
            z_ref[lo:lo + b, 0:lo] = -jnp.dot(d, t, precision=HI, preferred_element_type=jnp.float32)


def inverse_cholesky(a, b=128):
    n = a.shape[0]
    return pl.pallas_call(
        functools.partial(_kernel, n=n, b=b),
        out_shape=jax.ShapeDtypeStruct((n, n), jnp.float32),
        in_specs=[pl.BlockSpec(memory_space=pltpu.VMEM)],
        out_specs=pl.BlockSpec(memory_space=pltpu.VMEM),
        compiler_params=pltpu.CompilerParams(vmem_limit_bytes=48 * 1024 * 1024),
        cost_estimate=pl.CostEstimate(
            flops=2 * n * n * n, transcendentals=n, bytes_accessed=8 * n * n
        ),
    )(a)


def split3(x):
    hi = lax.reduce_precision(x, exponent_bits=8, mantissa_bits=7)
    rest = x - hi
    mid = lax.reduce_precision(rest, exponent_bits=8, mantissa_bits=7)
    lo = rest - mid
    return jnp.concatenate([hi, mid, lo]).astype(jnp.bfloat16)


def join3(parts):
    parts = parts.astype(jnp.float32).reshape(parts.shape[:-1] + (3, -1))
    return (parts[..., 0, :] + parts[..., 1, :]) + parts[..., 2, :]


def local(block_rows, inverse_factor, live_rows, shift):
    highest = lax.Precision.HIGHEST
    high = lax.Precision.HIGH
    groups = lax.axis_size("grp")
    rowcount = lax.axis_size("row")
    colcount = lax.axis_size("col")
    owners = groups * rowcount
    slab = PW // owners
    window = slab // colcount
    group_index = lax.axis_index("grp")
    row_index = lax.axis_index("row")
    col_index = lax.axis_index("col")
    blocks, padded, local_cols = block_rows.shape
    stacked = blocks * padded
    total = stacked * groups

    ordinal = jnp.arange(padded, dtype=jnp.int32)
    live_mask = (ordinal[None, :] < live_rows[:, None]).astype(jnp.float32)
    masked_factor = inverse_factor * live_mask[:, :, None] * live_mask[:, None, :]
    whitened = jnp.einsum(
        "bij,bjm->mbi", masked_factor, block_rows.astype(jnp.float32), precision=highest
    )
    whitened = whitened.astype(jnp.bfloat16).reshape(local_cols, stacked)

    shift_row = jnp.zeros((1, stacked), jnp.bfloat16).at[0, : 3 * shift.shape[0]].set(
        split3(shift)
    )
    every = lax.all_gather(
        jnp.concatenate([whitened, shift_row], axis=0), "grp", axis=0, tiled=False
    )
    shift_grp = join3(every[:, local_cols, : 3 * shift.shape[0]]).reshape(groups, NPAN, window)
    every = jnp.transpose(every[:, :local_cols], (1, 0, 2)).reshape(groups, NPAN, window, total)

    panel_shift_row = jnp.zeros((1, total), jnp.bfloat16).at[0, : 3 * groups * window].set(
        split3(shift_grp[:, 0].reshape(-1))
    )
    panel_w = jnp.concatenate([every[:, 0].reshape(groups * window, total), panel_shift_row], 0)
    col_w = lax.all_gather(every, "row", axis=0, tiled=False)
    panel_w = remote_gather(panel_w, "col", colcount, 0)
    panel_w, col_w = lax.optimization_barrier((panel_w, col_w))
    panel_w = lax.all_gather(panel_w, "row", axis=0, tiled=False)
    every, panel_w = lax.optimization_barrier((every, panel_w))
    shift_panel = join3(panel_w[:, :, groups * window, : 3 * groups * window])
    shift_panel = jnp.transpose(
        shift_panel.reshape(rowcount, colcount, groups, window), (2, 0, 1, 3)
    ).reshape(PW)
    panel_w = panel_w[:, :, : groups * window].reshape(rowcount, colcount, groups, window, total)
    panel_w = jnp.transpose(panel_w, (2, 0, 1, 3, 4)).reshape(PW, total)

    row_w = lax.dynamic_index_in_dim(every, group_index, 0, keepdims=False)
    row_w = lax.all_gather(row_w, "col", axis=0, tiled=False)
    row_w = jnp.transpose(row_w, (1, 0, 2, 3)).reshape(NPAN * colcount * window, total)

    col_w = jnp.transpose(col_w, (2, 1, 0, 3, 4)).reshape(NPAN * owners * window, total)

    panel_ids = jnp.arange(NPAN, dtype=jnp.int32)
    slab_ids = jnp.arange(slab, dtype=jnp.int32)
    owner_ids = jnp.arange(owners, dtype=jnp.int32)
    window_ids = jnp.arange(window, dtype=jnp.int32)
    own_owner = group_index * rowcount + row_index
    row_global = ((panel_ids[:, None] * owners + own_owner) * slab + slab_ids[None, :]).reshape(-1)
    col_global = (
        (panel_ids[:, None, None] * owners + owner_ids[None, :, None]) * slab
        + col_index * window
        + window_ids[None, None, :]
    ).reshape(-1)
    panel_ids_all = jnp.arange(PW, dtype=jnp.int32)
    shift_col = jnp.broadcast_to(
        shift.reshape(NPAN, 1, window), (NPAN, owners, window)
    ).reshape(-1)

    dims = (((1,), (1,)), ((), ()))
    f32 = jnp.float32
    diag_block = lax.dot_general(panel_w, panel_w, dims, preferred_element_type=f32)
    diag_block = diag_block + jnp.where(
        panel_ids_all[:, None] == panel_ids_all[None, :], shift_panel[None, :], 0.0
    )
    both_w = jnp.concatenate([row_w, col_w], axis=0)
    both_global = jnp.concatenate([row_global, col_global], axis=0)
    both_panel = lax.dot_general(both_w, panel_w, dims, preferred_element_type=f32)
    both_panel = both_panel + jnp.where(
        both_global[:, None] == panel_ids_all[None, :], shift_panel[None, :], 0.0
    )
    schur_tile = lax.dot_general(row_w, col_w, dims, preferred_element_type=f32)
    schur_tile = schur_tile + jnp.where(
        row_global[:, None] == col_global[None, :], shift_col[None, :], 0.0
    )

    inverse_factor_panel = inverse_cholesky(diag_block)
    solved = lax.dot_general(
        both_panel, inverse_factor_panel, dims, precision=high, preferred_element_type=f32
    )
    local_rows = row_global.shape[0]
    row_factor = solved[:local_rows]
    col_factor = solved[local_rows:]

    panel_piece = lax.dynamic_slice_in_dim(
        row_factor.reshape(local_rows, owners, slab), col_index * window, window, 2
    ).reshape(local_rows, owners * window)
    panel_cols_global = col_global.reshape(NPAN, -1)[0]
    finished = jnp.where(row_global[:, None] >= panel_cols_global[None, :], panel_piece, 0.0)

    boundary = PANELS * PW
    first_trailing = owners * window
    update = jnp.dot(
        row_factor, col_factor[first_trailing:].T, precision=high, preferred_element_type=f32
    )
    trailing = schur_tile[:, first_trailing:] - update
    trailing = jnp.where(row_global[:, None] >= boundary, trailing, 0.0)
    return jnp.concatenate([finished, trailing], axis=1)


def solution(mesh):
    in_specs = (
        P("grp", None, ("row", "col")),
        P("grp", None, None),
        P("grp"),
        P(("grp", "row", "col")),
    )
    out_specs = P(("grp", "row"), "col")
    return jax.shard_map(local, mesh=mesh, in_specs=in_specs, out_specs=out_specs, check_vma=False)
```

profile of v0, /device:TPU:1, one launch (start us, length us, event | category | flops | bytes accessed | tf_op | source)
XLA Modules:
  0.0 321.7 jit_solution(5757943086684914308)
XLA Ops:
  6.5 0.6 compare_reduce_fusion
  7.2 0.7 fusion.28
  7.8 0.7 compare_convert_fusion
  8.6 2.1 fusion.16
  11.1 0.7 broadcast_select_fusion.1
  11.8 10.5 %all-gather.2 = bf16[4,161,608]{2,1,0:T(8,128)(2,1)S(1)} all-gather(bf16[1,161,608]{2,1,0:T(8,128)(2,1)S(1)} %fusion.24), channel_id=2, replica_groups=mesh['grp'=4,'row'=4,'col'=16] {'grp'}, dimensions={0}, use_global_device_ids=true | all-gather | bytes 978880 | tf_op jit(solution)/shard_map/all_gather | solution.py:184
  22.8 1.7 all_gather_reshape.3
  24.6 0.8 reshape.297
  26.4 0.7 fusion.25.x_ref
  27.1 50.0 %shard_map.46 = bf16[16,17,2432]{2,1,0:T(8,128)(2,1)} custom-call(bf16[17,2432]{1,0:T(8,128)(2,1)} %fusion.25.x_ref), custom_call_target="tpu_custom_call" | custom-call | tf_op jit(solution)/shard_map/pallas_call | solution.py:45
  77.2 2.7 copy.41
  80.5 60.5 %all-gather.11.cloned.1.call-done = bf16[64,17,2432]{2,0,1:T(8,128)(2,1)} async-done(((bf16[16,17,2432]{2,0,1:T(8,128)(2,1)}), bf16[64,17,2432]{2,0,1:T(8,128)(2,1)}) %all-gather.11.cloned.1.call-update) | async-done | bytes 5292048 | tf_op jit(solution)/shard_map/all_gather | solution.py:197
  141.0 0.7 constant_dynamic-slice_fusion.1
  142.7 3.1 copy.43
  145.8 3.0 reshape.299
  148.8 2.8 slice.91
  151.5 6.2 %copy.45 = bf16[4,4,16,4,2432]{4,3,2,1,0:T(4,128)(2,1)} copy(bf16[4,4,16,4,2432]{4,2,1,3,0:T(8,128)(2,1)S(1)} %bitcast.43) | data formatting | bytes 9961472 | tf_op jit(solution)/shard_map/transpose | solution.py:204
  157.7 8.7 %reshape.301 = bf16[1024,2432]{1,0:T(8,128)(2,1)} reshape(bf16[4,4,16,4,2432]{4,3,2,1,0:T(4,128)(2,1)} %copy.45) | data formatting | bytes 9961472 | tf_op jit(solution)/shard_map/reshape | solution.py:204
  166.4 0.7 slice_convert_fusion
  167.7 11.0 %select_add_fusion.a_ref = f32[1024,1024]{1,0:T(8,128)} fusion(f32[1024]{0:T(1024)S(1)} %broadcast_in_dim.78, bf16[1024,2432]{1,0:T(8,128)(2,1)} %reshape.301), kind=kOutput, calls=%fused_computation.8 | convolution fusion | flops 5103419392 | bytes 9179136 | tf_op jit(solution)/shard_map/dot_general | solution.py:230
  178.6 87.7 %shard_map.47 = f32[1024,1024]{1,0:T(8,128)S(1)} custom-call(f32[1024,1024]{1,0:T(8,128)} %select_add_fusion.a_ref), custom_call_target="tpu_custom_call" | custom-call | flops 2147483648 | bytes 8388608 | tf_op jit(solution)/shard_map/pallas_call | solution.py:132
  266.3 1.9 copy-done.2
  268.3 3.1 copy.42
  271.4 3.0 reshape.298
  274.4 6.8 %fusion.39 = f32[640,640]{0,1:T(8,128)} fusion(bf16[640,2432]{1,0:T(8,128)(2,1)} %reshape.298, bf16[640,2432]{1,0:T(8,128)(2,1)} %reshape.299), kind=kOutput, calls=%fused_computation.76 | convolution fusion | flops 1992294400 | bytes 7864320 | tf_op jit(solution)/shard_map/dot_general | solution.py:240
  281.2 10.7 %fusion = f32[1280,1024]{1,0:T(8,128)S(1)} fusion(bf16[1024,2432]{1,0:T(8,128)(2,1)} %reshape.301, bf16[640,2432]{1,0:T(8,128)(2,1)S(1)} %copy-done.5, bf16[640,2432]{1,0:T(8,128)(2,1)S(1)} %copy-done.6), kind=kOutput, calls=%fused_computation | convolution fusion | flops 6387793920 | bytes 16449536 | tf_op jit(solution)/shard_map/dot_general | solution.py:236
  292.0 8.9 %fusion.4 = f32[1280,1024]{1,0:T(8,128)S(1)} fusion(f32[1024,1024]{1,0:T(8,128)S(1)} %copy-done.3, f32[1280,1024]{1,0:T(8,128)S(1)} %fusion, f32[1024]{0:T(1024)S(1)} %broadcast_in_dim.78, s32[1280]{0:T(1024)S(1)} %pad_add_fusion), kind=kOutput, calls=%fused_computation.4 | convolution fusion | flops 8056995840 | bytes 14689280 | tf_op jit(solution)/shard_map/dot_general | solution.py:246
  300.9 2.3 copy-done.4
  303.4 2.4 copy.48
  305.7 1.0 constant_dynamic-slice_fusion
  306.9 5.9 %fusion.13 = f32[640,576]{0,1:T(8,128)S(1)} fusion(f32[640,640]{0,1:T(8,128)} %fusion.39, f32[1280,1024]{1,0:T(8,128)} %copy-done.4, f32[576]{0:T(1024)S(1)} %slice.112, s32[640]{0:T(1024)S(1)} %add.143, s32[576]{0:T(1024)S(1)} %slice.111, pred[640]{0:T(1024)(128)(4,1)S(1)} %broadcast_compare_fusion), kind=kOutput, calls=%fused_computation.18 | convolution fusion | flops 2266767360 | bytes 7937664 | tf_op jit(solution)/shard_map/dot_general | solution.py:261
  313.0 1.7 copy.49
  (62 shorter events, 4.4 us)
Async XLA Ops:
  6.5 2.0 copy-start
  6.5 70.6 %all-gather.7.cloned.1.call-start = ((), (), s32[]{:S(2)}) async-start(), calls=%async_computation | async-start | bytes 3891200 | tf_op jit(solution)/shard_map/all_gather | solution.py:194
  24.5 116.5 %all-gather.11.cloned.1.call-start = ((), (), s32[]{:S(2)}) async-start(), calls=%async_computation.2 | async-start | bytes 6615040 | tf_op jit(solution)/shard_map/all_gather | solution.py:197
  25.4 116.4 %copy-start.7 = (f32[40]{0:T(128)S(1)}, f32[40]{0:T(128)}, u32[]{:S(2)}) copy-start(f32[40]{0:T(128)} %param.11) | copy-start | bytes 484
  79.9 188.4 %all-gather.9.cloned.1.call-start = ((), (), s32[]{:S(2)}) async-start(), calls=%async_computation.1 | async-start | bytes 3307520 | tf_op jit(solution)/shard_map/all_gather | solution.py:207
  266.3 1.9 copy-start.2
  274.4 6.8 %copy-start.5 = (bf16[640,2432]{1,0:T(8,128)(2,1)S(1)}, bf16[640,2432]{1,0:T(8,128)(2,1)}, u32[]{:S(2)}) copy-start(bf16[640,2432]{1,0:T(8,128)(2,1)} %reshape.299) | copy-start | bytes 9338884
  274.4 6.8 %copy-start.6 = (bf16[640,2432]{1,0:T(8,128)(2,1)S(1)}, bf16[640,2432]{1,0:T(8,128)(2,1)}, u32[]{:S(2)}) copy-start(bf16[640,2432]{1,0:T(8,128)(2,1)} %reshape.298) | copy-start | bytes 9338884
  281.2 10.8 %copy-start.3 = (f32[1024,1024]{1,0:T(8,128)S(1)}, f32[1024,1024]{1,0:T(8,128)}, u32[]{:S(2)}) copy-start(f32[1024,1024]{1,0:T(8,128)} %copy-done.2) | copy-start | bytes 12582916
  300.9 2.3 copy-start.4
  306.9 7.7 %copy-start.1 = (bf16[2,304,160]{1,2,0:T(8,128)(2,1)S(1)}, bf16[2,304,160]{1,2,0:T(8,128)(2,1)}, u32[]{:S(2)}) copy-start(bf16[2,304,160]{1,2,0:T(8,128)(2,1)} %param.8) | copy-start | bytes 583684
Sparse Core Ops, SparseCore 0:
  24.7 43.8 all-gather.6
  80.0 60.9 all-gather.10
  143.6 90.0 all-gather.8
where the time goes:
time: 326 us; the launch traced here: 322 us
  Pallas kernels  138 us (42%)
  waiting for transfers between devices  60.6 us (19%)
  local copies, waits for them, and re-layouts  47.6 us (15%)
  matrix products  45.4 us (14%)
  between operations  13.9 us (4%)
  blocking collectives  10.5 us (3%)
  other arithmetic  5.36 us (2%)
    pallas_call x1, Pallas kernels, inverse_cholesky(): pl.pallas_call(functools.partial(_kernel, n=n, b=b), out_shape=jax.ShapeD...  87.7 us
    all_gather x1, waiting for transfers between devices, local(): panel_w = lax.all_gather(panel_w, 'row', axis=0, tiled=False)  60.5 us
    pallas_call x1, Pallas kernels, remote_gather(): pl.pallas_call(functools.partial(_gather_kernel, axis=axis, count=count),...  50 us
    dot_general x1, matrix products, local(): lax.dot_general(panel_w, panel_w, dims, preferred_element_type=f32)  11 us
    dot_general x1, matrix products, local(): lax.dot_general(both_w, panel_w, dims, preferred_element_type=f32)  10.7 us
    all_gather x1, blocking collectives, local(): lax.all_gather(jnp.concatenate([whitened, shift_row], axis=0), 'grp', axi...  10.5 us
    dot_general x1, matrix products, local(): lax.dot_general(both_panel, inverse_factor_panel, dims, precision=high, p...  8.88 us
    reshape x1, local copies, waits for them, and re-layouts, local(): panel_w = jnp.transpose(panel_w, (2, 0, 1, 3, 4)).reshape(PW, total)  8.71 us
  transfers between devices with their start and end apart: 3, of which 1 were waited for; matrix products, arithmetic and copies ran while one was open for 12% of the time, Pallas kernels for 43%

commit v1 on v0

--- a/solution.py
+++ b/solution.py
@@ -10,7 +10,7 @@
 PW = 1024
 PANELS = 1
 NPAN = 10
-HI = lax.Precision.HIGHEST
+HI = lax.Precision.HIGH
 MESH = pl.DeviceIdType.MESH
 
 

time: 326 us -> 319 us (0.979)
  Pallas kernels: 138 us -> 129 us
    pallas_call x1, Pallas kernels: 87.7 us -> 79 us  [inverse_cholesky(): pl.pallas_call(functools.partial(_kernel, n=n, b=b), out_shape=jax.ShapeD...]
  transfers between devices with their start and end apart: 3 -> 3, of which waited for: 1 -> 1; matrix products, arithmetic and copies ran while one was open for 12% -> 13% of each run, Pallas kernels for 43% -> 41%
where the time goes in v1:
time: 319 us; the launch traced here: 313 us
  Pallas kernels  129 us (40%)
  waiting for transfers between devices  61.1 us (19%)
  local copies, waits for them, and re-layouts  48.1 us (15%)
  matrix products  45.4 us (14%)
  between operations  13.7 us (4%)
  blocking collectives  10.5 us (3%)
  other arithmetic  5.36 us (2%)
    pallas_call x1, Pallas kernels, inverse_cholesky(): pl.pallas_call(functools.partial(_kernel, n=n, b=b), out_shape=jax.ShapeD...  79 us
    all_gather x1, waiting for transfers between devices, local(): panel_w = lax.all_gather(panel_w, 'row', axis=0, tiled=False)  61.1 us
    pallas_call x1, Pallas kernels, remote_gather(): pl.pallas_call(functools.partial(_gather_kernel, axis=axis, count=count),...  50 us
    dot_general x1, matrix products, local(): lax.dot_general(panel_w, panel_w, dims, preferred_element_type=f32)  11 us
    dot_general x1, matrix products, local(): lax.dot_general(both_w, panel_w, dims, preferred_element_type=f32)  10.7 us
    all_gather x1, blocking collectives, local(): lax.all_gather(jnp.concatenate([whitened, shift_row], axis=0), 'grp', axi...  10.5 us
    dot_general x1, matrix products, local(): lax.dot_general(both_panel, inverse_factor_panel, dims, precision=high, p...  8.88 us
    reshape x1, local copies, waits for them, and re-layouts, local(): panel_w = jnp.transpose(panel_w, (2, 0, 1, 3, 4)).reshape(PW, total)  8.71 us
  transfers between devices with their start and end apart: 3, of which 1 were waited for; matrix products, arithmetic and copies ran while one was open for 13% of the time, Pallas kernels for 41%

profile of v1, /device:TPU:1, one launch (start us, length us, event | category | flops | bytes accessed | tf_op | source)
XLA Modules:
  0.0 313.2 jit_solution(6702180417602314429)
XLA Ops:
  6.5 0.6 compare_reduce_fusion
  7.2 0.7 fusion.28
  7.8 0.7 compare_convert_fusion
  8.6 2.1 fusion.16
  11.1 0.7 broadcast_select_fusion.1
  11.8 10.5 %all-gather.2 = bf16[4,161,608]{2,1,0:T(8,128)(2,1)S(1)} all-gather(bf16[1,161,608]{2,1,0:T(8,128)(2,1)S(1)} %fusion.24), channel_id=2, replica_groups=mesh['grp'=4,'row'=4,'col'=16] {'grp'}, dimensions={0}, use_global_device_ids=true | all-gather | bytes 978880 | tf_op jit(solution)/shard_map/all_gather | solution.py:184
  22.8 1.7 all_gather_reshape.3
  24.6 0.8 reshape.297
  26.4 0.7 fusion.25.x_ref
  27.1 50.0 %shard_map.46 = bf16[16,17,2432]{2,1,0:T(8,128)(2,1)} custom-call(bf16[17,2432]{1,0:T(8,128)(2,1)} %fusion.25.x_ref), custom_call_target="tpu_custom_call" | custom-call | tf_op jit(solution)/shard_map/pallas_call | solution.py:45
  77.2 2.7 copy.41
  79.9 61.1 %all-gather.11.cloned.1.call-done = bf16[64,17,2432]{2,0,1:T(8,128)(2,1)} async-done(((bf16[16,17,2432]{2,0,1:T(8,128)(2,1)}), bf16[64,17,2432]{2,0,1:T(8,128)(2,1)}) %all-gather.11.cloned.1.call-update) | async-done | bytes 5292048 | tf_op jit(solution)/shard_map/all_gather | solution.py:197
  141.0 0.7 constant_dynamic-slice_fusion.1
  142.7 3.1 copy.43
  145.8 3.5 %reshape.299 = bf16[640,2432]{1,0:T(8,128)(2,1)} reshape(bf16[10,4,4,4,2432]{4,3,2,1,0:T(4,128)(2,1)S(1)} %copy.43) | data formatting | bytes 6225920 | tf_op jit(solution)/shard_map/reshape | solution.py:210
  149.3 2.8 slice.91
  152.1 6.2 %copy.45 = bf16[4,4,16,4,2432]{4,3,2,1,0:T(4,128)(2,1)} copy(bf16[4,4,16,4,2432]{4,2,1,3,0:T(8,128)(2,1)S(1)} %bitcast.43) | data formatting | bytes 9961472 | tf_op jit(solution)/shard_map/transpose | solution.py:204
  158.2 8.7 %reshape.301 = bf16[1024,2432]{1,0:T(8,128)(2,1)} reshape(bf16[4,4,16,4,2432]{4,3,2,1,0:T(4,128)(2,1)} %copy.45) | data formatting | bytes 9961472 | tf_op jit(solution)/shard_map/reshape | solution.py:204
  166.9 0.7 slice_convert_fusion
  168.2 11.0 %select_add_fusion.a_ref = f32[1024,1024]{1,0:T(8,128)} fusion(f32[1024]{0:T(1024)S(1)} %broadcast_in_dim.78, bf16[1024,2432]{1,0:T(8,128)(2,1)} %reshape.301), kind=kOutput, calls=%fused_computation.8 | convolution fusion | flops 5103419392 | bytes 9179136 | tf_op jit(solution)/shard_map/dot_general | solution.py:230
  179.2 79.0 %shard_map.47 = f32[1024,1024]{1,0:T(8,128)S(1)} custom-call(f32[1024,1024]{1,0:T(8,128)} %select_add_fusion.a_ref), custom_call_target="tpu_custom_call" | custom-call | flops 2147483648 | bytes 8388608 | tf_op jit(solution)/shard_map/pallas_call | solution.py:132
  258.2 1.9 copy-done.2
  260.1 3.1 copy.42
  263.2 3.0 reshape.298
  266.3 6.8 %fusion.39 = f32[640,640]{0,1:T(8,128)} fusion(bf16[640,2432]{1,0:T(8,128)(2,1)} %reshape.298, bf16[640,2432]{1,0:T(8,128)(2,1)} %reshape.299), kind=kOutput, calls=%fused_computation.76 | convolution fusion | flops 1992294400 | bytes 7864320 | tf_op jit(solution)/shard_map/dot_general | solution.py:240
  273.1 10.7 %fusion = f32[1280,1024]{1,0:T(8,128)S(1)} fusion(bf16[1024,2432]{1,0:T(8,128)(2,1)} %reshape.301, bf16[640,2432]{1,0:T(8,128)(2,1)S(1)} %copy-done.5, bf16[640,2432]{1,0:T(8,128)(2,1)S(1)} %copy-done.6), kind=kOutput, calls=%fused_computation | convolution fusion | flops 6387793920 | bytes 16449536 | tf_op jit(solution)/shard_map/dot_general | solution.py:236
  283.8 8.9 %fusion.4 = f32[1280,1024]{1,0:T(8,128)S(1)} fusion(f32[1024,1024]{1,0:T(8,128)S(1)} %copy-done.3, f32[1280,1024]{1,0:T(8,128)S(1)} %fusion, f32[1024]{0:T(1024)S(1)} %broadcast_in_dim.78, s32[1280]{0:T(1024)S(1)} %pad_add_fusion), kind=kOutput, calls=%fused_computation.4 | convolution fusion | flops 8056995840 | bytes 14689280 | tf_op jit(solution)/shard_map/dot_general | solution.py:246
  292.7 2.3 copy-done.4
  295.2 2.3 copy.48
  297.5 1.0 constant_dynamic-slice_fusion
  298.7 5.9 %fusion.13 = f32[640,576]{0,1:T(8,128)S(1)} fusion(f32[640,640]{0,1:T(8,128)} %fusion.39, f32[1280,1024]{1,0:T(8,128)} %copy-done.4, f32[576]{0:T(1024)S(1)} %slice.112, s32[640]{0:T(1024)S(1)} %add.143, s32[576]{0:T(1024)S(1)} %slice.111, pred[640]{0:T(1024)(128)(4,1)S(1)} %broadcast_compare_fusion), kind=kOutput, calls=%fused_computation.18 | convolution fusion | flops 2266767360 | bytes 7937664 | tf_op jit(solution)/shard_map/dot_general | solution.py:261
  304.7 1.7 copy.49
  (62 shorter events, 3.9 us)
Async XLA Ops:
  6.5 2.0 copy-start
  6.5 70.6 %all-gather.7.cloned.1.call-start = ((), (), s32[]{:S(2)}) async-start(), calls=%async_computation | async-start | bytes 3891200 | tf_op jit(solution)/shard_map/all_gather | solution.py:194
  24.5 116.5 %all-gather.11.cloned.1.call-start = ((), (), s32[]{:S(2)}) async-start(), calls=%async_computation.2 | async-start | bytes 6615040 | tf_op jit(solution)/shard_map/all_gather | solution.py:197
  25.4 116.4 %copy-start.7 = (f32[40]{0:T(128)S(1)}, f32[40]{0:T(128)}, u32[]{:S(2)}) copy-start(f32[40]{0:T(128)} %param.11) | copy-start | bytes 484
  79.9 180.2 %all-gather.9.cloned.1.call-start = ((), (), s32[]{:S(2)}) async-start(), calls=%async_computation.1 | async-start | bytes 3307520 | tf_op jit(solution)/shard_map/all_gather | solution.py:207
  258.2 1.9 copy-start.2
  266.3 6.8 %copy-start.5 = (bf16[640,2432]{1,0:T(8,128)(2,1)S(1)}, bf16[640,2432]{1,0:T(8,128)(2,1)}, u32[]{:S(2)}) copy-start(bf16[640,2432]{1,0:T(8,128)(2,1)} %reshape.299) | copy-start | bytes 9338884
  266.3 6.8 %copy-start.6 = (bf16[640,2432]{1,0:T(8,128)(2,1)S(1)}, bf16[640,2432]{1,0:T(8,128)(2,1)}, u32[]{:S(2)}) copy-start(bf16[640,2432]{1,0:T(8,128)(2,1)} %reshape.298) | copy-start | bytes 9338884
  273.1 10.7 %copy-start.3 = (f32[1024,1024]{1,0:T(8,128)S(1)}, f32[1024,1024]{1,0:T(8,128)}, u32[]{:S(2)}) copy-start(f32[1024,1024]{1,0:T(8,128)} %copy-done.2) | copy-start | bytes 12582916
  292.7 2.3 copy-start.4
  298.7 7.8 %copy-start.1 = (bf16[2,304,160]{1,2,0:T(8,128)(2,1)S(1)}, bf16[2,304,160]{1,2,0:T(8,128)(2,1)}, u32[]{:S(2)}) copy-start(bf16[2,304,160]{1,2,0:T(8,128)(2,1)} %param.8) | copy-start | bytes 583684
Sparse Core Ops, SparseCore 0:
  24.7 43.8 all-gather.6
  80.0 60.9 all-gather.10
  143.6 90.1 all-gather.8

commit v2 on v1

--- a/solution.py
+++ b/solution.py
@@ -14,21 +14,22 @@
 MESH = pl.DeviceIdType.MESH
 
 
-def _gather_kernel(x_ref, out_ref, local_sem, send_sem, recv_sem, *, axis, count):
+def _gather_kernel(x_ref, out_ref, local_sem, send_sem, recv_sem, *, axis, count, position):
     me = lax.axis_index(axis)
+    slot = out_ref.at[(slice(None),) * position + (me,)]
     barrier = pltpu.get_barrier_semaphore()
     for step in range(1, count):
         peer = lax.rem(me + step, count)
         pl.semaphore_signal(barrier, inc=1, device_id={axis: peer}, device_id_type=MESH)
     pl.semaphore_wait(barrier, count - 1)
-    own = pltpu.make_async_copy(x_ref, out_ref.at[me], local_sem)
+    own = pltpu.make_async_copy(x_ref, slot, local_sem)
     own.start()
     copies = []
     for step in range(1, count):
         peer = lax.rem(me + step, count)
         copy = pltpu.make_async_remote_copy(
             src_ref=x_ref,
-            dst_ref=out_ref.at[me],
+            dst_ref=slot,
             send_sem=send_sem.at[step],
             recv_sem=recv_sem.at[step],
             device_id={axis: peer},
@@ -41,10 +42,12 @@
         copy.wait()
 
 
-def remote_gather(x, axis, count, collective_id):
+def remote_gather(x, axis, count, collective_id, position=0):
     return pl.pallas_call(
-        functools.partial(_gather_kernel, axis=axis, count=count),
-        out_shape=jax.ShapeDtypeStruct((count,) + x.shape, x.dtype),
+        functools.partial(_gather_kernel, axis=axis, count=count, position=position),
+        out_shape=jax.ShapeDtypeStruct(
+            x.shape[:position] + (count,) + x.shape[position:], x.dtype
+        ),
         in_specs=[pl.BlockSpec(memory_space=pl.ANY)],
         out_specs=pl.BlockSpec(memory_space=pl.ANY),
         scratch_shapes=[
@@ -146,7 +149,7 @@
     rest = x - hi
     mid = lax.reduce_precision(rest, exponent_bits=8, mantissa_bits=7)
     lo = rest - mid
-    return jnp.concatenate([hi, mid, lo]).astype(jnp.bfloat16)
+    return jnp.concatenate([hi, mid, lo], axis=-1).astype(jnp.bfloat16)
 
 
 def join3(parts):
@@ -187,21 +190,17 @@
     shift_grp = join3(every[:, local_cols, : 3 * shift.shape[0]]).reshape(groups, NPAN, window)
     every = jnp.transpose(every[:, :local_cols], (1, 0, 2)).reshape(groups, NPAN, window, total)
 
-    panel_shift_row = jnp.zeros((1, total), jnp.bfloat16).at[0, : 3 * groups * window].set(
-        split3(shift_grp[:, 0].reshape(-1))
-    )
-    panel_w = jnp.concatenate([every[:, 0].reshape(groups * window, total), panel_shift_row], 0)
+    panel_shift_row = jnp.zeros((groups, 1, total), jnp.bfloat16).at[:, 0, : 3 * window].set(
+        split3(shift_grp[:, 0])
+    )
+    panel_w = jnp.concatenate([every[:, 0], panel_shift_row], 1)
     col_w = lax.all_gather(every, "row", axis=0, tiled=False)
-    panel_w = remote_gather(panel_w, "col", colcount, 0)
+    panel_w = remote_gather(panel_w, "col", colcount, 0, position=1)
     panel_w, col_w = lax.optimization_barrier((panel_w, col_w))
-    panel_w = lax.all_gather(panel_w, "row", axis=0, tiled=False)
+    panel_w = lax.all_gather(panel_w, "row", axis=1, tiled=False)
     every, panel_w = lax.optimization_barrier((every, panel_w))
-    shift_panel = join3(panel_w[:, :, groups * window, : 3 * groups * window])
-    shift_panel = jnp.transpose(
-        shift_panel.reshape(rowcount, colcount, groups, window), (2, 0, 1, 3)
-    ).reshape(PW)
-    panel_w = panel_w[:, :, : groups * window].reshape(rowcount, colcount, groups, window, total)
-    panel_w = jnp.transpose(panel_w, (2, 0, 1, 3, 4)).reshape(PW, total)
+    shift_panel = join3(panel_w[:, :, :, window, : 3 * window]).reshape(PW)
+    panel_w = panel_w[:, :, :, :window].reshape(PW, total)
 
     row_w = lax.dynamic_index_in_dim(every, group_index, 0, keepdims=False)
     row_w = lax.all_gather(row_w, "col", axis=0, tiled=False)

time: 319 us -> 432 us (1.35)
  local copies, waits for them, and re-layouts: 48.1 us -> 108 us
  waiting for transfers between devices: 61.1 us -> 101 us
  Pallas kernels: 129 us -> 142 us
    optimization_barrier x1, local copies, waits for them, and re-layouts: 2.7 us -> 63 us  [local(): every, panel_w = lax.optimization_barrier((every, panel_w))]
    all_gather x1, waiting for transfers between devices: 61.1 us -> 101 us  [local(): panel_w = lax.all_gather(panel_w, 'row', axis=1, tiled=False)]
    pallas_call x1, Pallas kernels: 50 us -> 63.3 us  [remote_gather(): pl.pallas_call(functools.partial(_gather_kernel, axis=axis, count=count,...]
    transpose x2 -> x0, local copies, waits for them, and re-layouts: 6.33 us -> none  [the longest x1 6.16 us: local(): panel_w = jnp.transpose(panel_w, (2, 0, 1, 3, 4)).reshape(PW, total)]
    slice x3 -> x2, local copies, waits for them, and re-layouts: 2.82 us -> 8.84 us  [the longest x1 8.02 us: local(): panel_w = panel_w[:, :, :, :window].reshape(PW, total)]
  transfers between devices with their start and end apart: 3 -> 3, of which waited for: 1 -> 1; matrix products, arithmetic and copies ran while one was open for 13% -> 24% of each run, Pallas kernels for 41% -> 33%
where the time goes in v2:
time: 432 us; the launch traced here: 425 us
  Pallas kernels  142 us (33%)
  local copies, waits for them, and re-layouts  108 us (25%)
  waiting for transfers between devices  101 us (23%)
  matrix products  45.3 us (10%)
  between operations  13.6 us (3%)
  blocking collectives  10.5 us (2%)
    all_gather x1, waiting for transfers between devices, local(): panel_w = lax.all_gather(panel_w, 'row', axis=1, tiled=False)  101 us
    pallas_call x1, Pallas kernels, inverse_cholesky(): pl.pallas_call(functools.partial(_kernel, n=n, b=b), out_shape=jax.ShapeD...  79 us
    pallas_call x1, Pallas kernels, remote_gather(): pl.pallas_call(functools.partial(_gather_kernel, axis=axis, count=count,...  63.3 us
    optimization_barrier x1, local copies, waits for them, and re-layouts, local(): every, panel_w = lax.optimization_barrier((every, panel_w))  63 us
    dot_general x1, matrix products, local(): lax.dot_general(panel_w, panel_w, dims, preferred_element_type=f32)  10.9 us
    dot_general x1, matrix products, local(): lax.dot_general(both_w, panel_w, dims, preferred_element_type=f32)  10.7 us
    all_gather x1, blocking collectives, local(): lax.all_gather(jnp.concatenate([whitened, shift_row], axis=0), 'grp', axi...  10.5 us
    dot_general x1, matrix products, local(): lax.dot_general(both_panel, inverse_factor_panel, dims, precision=high, p...  8.88 us
  transfers between devices with their start and end apart: 3, of which 1 were waited for; matrix products, arithmetic and copies ran while one was open for 24% of the time, Pallas kernels for 33%

profile of v2, /device:TPU:1, one launch (start us, length us, event | category | flops | bytes accessed | tf_op | source)
XLA Modules:
  0.0 424.7 jit_solution(6409309767816285019)
XLA Ops:
  6.5 0.6 compare_reduce_fusion
  7.2 0.7 fusion.27
  7.8 0.7 compare_convert_fusion
  8.6 2.1 fusion.16
  11.1 0.7 broadcast_select_fusion
  11.8 10.5 %all-gather.2 = bf16[4,161,608]{2,1,0:T(8,128)(2,1)S(1)} all-gather(bf16[1,161,608]{2,1,0:T(8,128)(2,1)S(1)} %fusion.23), channel_id=2, replica_groups=mesh['grp'=4,'row'=4,'col'=16] {'grp'}, dimensions={0}, use_global_device_ids=true | all-gather | bytes 978880 | tf_op jit(solution)/shard_map/all_gather | solution.py:187
  22.4 0.4 copy.36
  22.8 1.7 all_gather_reshape.3
  24.6 0.8 reshape.303
  25.7 0.7 pad_maximum_fusion.1.x_ref
  26.5 63.3 %shard_map.46 = bf16[4,16,5,2432]{3,2,1,0:T(8,128)(2,1)} custom-call(bf16[4,5,2432]{2,1,0:T(8,128)(2,1)} %pad_maximum_fusion.1.x_ref), custom_call_target="tpu_custom_call" | custom-call | tf_op jit(solution)/shard_map/pallas_call | solution.py:46
  89.9 100.9 %all-gather.11.cloned.1.call-done = bf16[4,64,5,2432]{3,2,1,0:T(8,128)(2,1)} async-done(((bf16[4,16,5,2432]{3,2,1,0:T(8,128)(2,1)}), bf16[4,64,5,2432]{3,2,1,0:T(8,128)(2,1)}) %all-gather.11.cloned.1.call-update) | async-done | bytes 6225936 | tf_op jit(solution)/shard_map/all_gather | solution.py:200
  190.7 0.7 constant_dynamic-slice_fusion.1
  192.4 3.1 copy.40
  195.6 3.4 reshape.305
  199.0 63.0 %copy.41 = bf16[4,4,16,5,2432]{2,1,4,0,3:T(4,128)(2,1)} copy(bf16[4,4,16,5,2432]{4,3,2,1,0:T(8,128)(2,1)} %bitcast.35) | data formatting | bytes 12451840 | tf_op jit(solution)/shard_map/optimization_barrier | solution.py:201
  262.1 8.0 %slice.98 = bf16[4,4,16,4,2432]{4,3,2,1,0:T(4,128)(2,1)} slice(bf16[4,4,16,5,2432]{4,3,2,1,0:T(8,128)(2,1)} %bitcast.36), slice={[0:4], [0:4], [0:16], [0:4], [0:2432]} | slice | bytes 9961472 | tf_op jit(solution)/shard_map/slice | solution.py:203
  270.1 0.8 slice.114
  271.2 8.8 %reshape.306 = bf16[1024,2432]{1,0:T(8,128)(2,1)} reshape(bf16[4,4,16,4,2432]{4,3,2,1,0:T(4,128)(2,1)} %slice.98) | data formatting | bytes 9961472 | tf_op jit(solution)/shard_map/reshape | solution.py:203
  280.0 10.9 %select_add_fusion.a_ref = f32[1024,1024]{1,0:T(8,128)} fusion(f32[1024]{0:T(1024)S(1)} %add.165, bf16[1024,2432]{1,0:T(8,128)(2,1)} %reshape.306), kind=kOutput, calls=%fused_computation.8 | convolution fusion | flops 5103419392 | bytes 9179136 | tf_op jit(solution)/shard_map/dot_general | solution.py:229
  290.9 79.0 %shard_map.47 = f32[1024,1024]{1,0:T(8,128)S(1)} custom-call(f32[1024,1024]{1,0:T(8,128)} %select_add_fusion.a_ref), custom_call_target="tpu_custom_call" | custom-call | flops 2147483648 | bytes 8388608 | tf_op jit(solution)/shard_map/pallas_call | solution.py:135
  369.9 2.0 copy-done.2
  371.9 3.1 copy.39
  375.0 3.0 reshape.304
  378.0 6.8 %fusion.34 = f32[640,640]{0,1:T(8,128)} fusion(bf16[640,2432]{1,0:T(8,128)(2,1)} %reshape.304, bf16[640,2432]{1,0:T(8,128)(2,1)} %reshape.305), kind=kOutput, calls=%fused_computation.71 | convolution fusion | flops 1992294400 | bytes 7864320 | tf_op jit(solution)/shard_map/dot_general | solution.py:239
  384.9 10.7 %fusion = f32[1280,1024]{1,0:T(8,128)S(1)} fusion(bf16[1024,2432]{1,0:T(8,128)(2,1)} %reshape.306, bf16[640,2432]{1,0:T(8,128)(2,1)S(1)} %copy-done.5, bf16[640,2432]{1,0:T(8,128)(2,1)S(1)} %copy-done.6), kind=kOutput, calls=%fused_computation | convolution fusion | flops 6387793920 | bytes 16449536 | tf_op jit(solution)/shard_map/dot_general | solution.py:235
  395.6 8.9 %fusion.4 = f32[1280,1024]{1,0:T(8,128)S(1)} fusion(f32[1024,1024]{1,0:T(8,128)S(1)} %copy-done.3, f32[1280,1024]{1,0:T(8,128)S(1)} %fusion, f32[1024]{0:T(1024)S(1)} %add.165, s32[1280]{0:T(1024)S(1)} %pad_add_fusion), kind=kOutput, calls=%fused_computation.4 | convolution fusion | flops 8056995840 | bytes 14689280 | tf_op jit(solution)/shard_map/dot_general | solution.py:245
  404.5 2.3 copy-done.4
  406.9 2.1 copy.43
  409.0 1.0 constant_dynamic-slice_fusion
  410.2 5.9 %fusion.13 = f32[640,576]{0,1:T(8,128)S(1)} fusion(f32[640,640]{0,1:T(8,128)} %fusion.34, f32[1280,1024]{1,0:T(8,128)} %copy-done.4, f32[576]{0:T(1024)S(1)} %slice.120, s32[640]{0:T(1024)S(1)} %add.149, s32[576]{0:T(1024)S(1)} %slice.119, pred[640]{0:T(1024)(128)(4,1)S(1)} %broadcast_compare_fusion), kind=kOutput, calls=%fused_computation.18 | convolution fusion | flops 2266767360 | bytes 7937664 | tf_op jit(solution)/shard_map/dot_general | solution.py:260
  416.2 1.7 copy.44
  (57 shorter events, 2.6 us)
Async XLA Ops:
  6.5 2.0 copy-start
  6.5 83.2 %all-gather.7.cloned.1.call-start = ((), (), s32[]{:S(2)}) async-start(), calls=%async_computation | async-start | bytes 3891200 | tf_op jit(solution)/shard_map/all_gather | solution.py:197
  24.5 167.0 %copy-start.7 = (f32[40]{0:T(128)S(1)}, f32[40]{0:T(128)}, u32[]{:S(2)}) copy-start(f32[40]{0:T(128)} %param.11) | copy-start | bytes 484
  24.5 166.2 %all-gather.11.cloned.1.call-start = ((), (), s32[]{:S(2)}) async-start(), calls=%async_computation.2 | async-start | bytes 12451840 | tf_op jit(solution)/shard_map/all_gather | solution.py:200
  89.8 282.1 %all-gather.9.cloned.1.call-start = ((), (), s32[]{:S(2)}) async-start(), calls=%async_computation.1 | async-start | bytes 3307520 | tf_op jit(solution)/shard_map/all_gather | solution.py:206
  369.9 2.0 copy-start.2
  378.0 6.8 %copy-start.5 = (bf16[640,2432]{1,0:T(8,128)(2,1)S(1)}, bf16[640,2432]{1,0:T(8,128)(2,1)}, u32[]{:S(2)}) copy-start(bf16[640,2432]{1,0:T(8,128)(2,1)} %reshape.305) | copy-start | bytes 9338884
  378.0 6.8 %copy-start.6 = (bf16[640,2432]{1,0:T(8,128)(2,1)S(1)}, bf16[640,2432]{1,0:T(8,128)(2,1)}, u32[]{:S(2)}) copy-start(bf16[640,2432]{1,0:T(8,128)(2,1)} %reshape.304) | copy-start | bytes 9338884
  384.8 10.7 %copy-start.3 = (f32[1024,1024]{1,0:T(8,128)S(1)}, f32[1024,1024]{1,0:T(8,128)}, u32[]{:S(2)}) copy-start(f32[1024,1024]{1,0:T(8,128)} %copy-done.2) | copy-start | bytes 12582916
  404.5 2.3 copy-start.4
  410.2 7.7 %copy-start.1 = (bf16[2,304,160]{1,2,0:T(8,128)(2,1)S(1)}, bf16[2,304,160]{1,2,0:T(8,128)(2,1)}, u32[]{:S(2)}) copy-start(bf16[2,304,160]{1,2,0:T(8,128)(2,1)} %param.8) | copy-start | bytes 583684
Sparse Core Ops, SparseCore 0:
  24.7 43.8 all-gather.6
  89.9 100.7 all-gather.10
  193.4 90.5 all-gather.8

commit v3 on v1

--- a/solution.py
+++ b/solution.py
@@ -195,7 +195,8 @@
     panel_w = remote_gather(panel_w, "col", colcount, 0)
     panel_w, col_w = lax.optimization_barrier((panel_w, col_w))
     panel_w = lax.all_gather(panel_w, "row", axis=0, tiled=False)
-    every, panel_w = lax.optimization_barrier((every, panel_w))
+    col_w = jnp.transpose(col_w, (2, 1, 0, 3, 4)).reshape(NPAN * owners * window, total)
+    every, panel_w, col_w = lax.optimization_barrier((every, panel_w, col_w))
     shift_panel = join3(panel_w[:, :, groups * window, : 3 * groups * window])
     shift_panel = jnp.transpose(
         shift_panel.reshape(rowcount, colcount, groups, window), (2, 0, 1, 3)
@@ -206,8 +207,6 @@
     row_w = lax.dynamic_index_in_dim(every, group_index, 0, keepdims=False)
     row_w = lax.all_gather(row_w, "col", axis=0, tiled=False)
     row_w = jnp.transpose(row_w, (1, 0, 2, 3)).reshape(NPAN * colcount * window, total)
-
-    col_w = jnp.transpose(col_w, (2, 1, 0, 3, 4)).reshape(NPAN * owners * window, total)
 
     panel_ids = jnp.arange(NPAN, dtype=jnp.int32)
     slab_ids = jnp.arange(slab, dtype=jnp.int32)

time: 319 us -> 313 us (0.981)
  waiting for transfers between devices: 61.1 us -> 54.5 us
    all_gather x1, waiting for transfers between devices: 61.1 us -> 54.4 us  [local(): panel_w = lax.all_gather(panel_w, 'row', axis=0, tiled=False)]
  transfers between devices with their start and end apart: 3 -> 3, of which waited for: 1 -> 1; matrix products, arithmetic and copies ran while one was open for 13% -> 13% of each run, Pallas kernels for 41% -> 42%
where the time goes in v3:
time: 313 us; the launch traced here: 308 us
  Pallas kernels  129 us (41%)
  waiting for transfers between devices  54.5 us (17%)
  local copies, waits for them, and re-layouts  49.1 us (16%)
  matrix products  45.4 us (15%)
  between operations  13.7 us (4%)
  blocking collectives  10.5 us (3%)
  other arithmetic  5.56 us (2%)
    pallas_call x1, Pallas kernels, inverse_cholesky(): pl.pallas_call(functools.partial(_kernel, n=n, b=b), out_shape=jax.ShapeD...  79 us
    all_gather x1, waiting for transfers between devices, local(): panel_w = lax.all_gather(panel_w, 'row', axis=0, tiled=False)  54.4 us
    pallas_call x1, Pallas kernels, remote_gather(): pl.pallas_call(functools.partial(_gather_kernel, axis=axis, count=count),...  50 us
    dot_general x1, matrix products, local(): lax.dot_general(panel_w, panel_w, dims, preferred_element_type=f32)  10.9 us
    dot_general x1, matrix products, local(): lax.dot_general(both_w, panel_w, dims, preferred_element_type=f32)  10.7 us
    all_gather x1, blocking collectives, local(): lax.all_gather(jnp.concatenate([whitened, shift_row], axis=0), 'grp', axi...  10.5 us
    dot_general x1, matrix products, local(): lax.dot_general(both_panel, inverse_factor_panel, dims, precision=high, p...  8.88 us
    reshape x1, local copies, waits for them, and re-layouts, local(): panel_w = jnp.transpose(panel_w, (2, 0, 1, 3, 4)).reshape(PW, total)  8.75 us
  transfers between devices with their start and end apart: 3, of which 1 were waited for; matrix products, arithmetic and copies ran while one was open for 13% of the time, Pallas kernels for 42%

profile of v3, /device:TPU:1, one launch (start us, length us, event | category | flops | bytes accessed | tf_op | source)
XLA Modules:
  0.0 307.8 jit_solution(16702222821263868281)
XLA Ops:
  6.5 0.7 compare_reduce_fusion
  7.9 0.7 compare_convert_fusion
  8.6 2.1 fusion.16
  11.1 0.7 broadcast_select_fusion.1
  11.9 10.5 %all-gather.2 = bf16[4,161,608]{2,1,0:T(8,128)(2,1)S(1)} all-gather(bf16[1,161,608]{2,1,0:T(8,128)(2,1)S(1)} %fusion.24), channel_id=2, replica_groups=mesh['grp'=4,'row'=4,'col'=16] {'grp'}, dimensions={0}, use_global_device_ids=true | all-gather | bytes 978880 | tf_op jit(solution)/shard_map/all_gather | solution.py:184
  22.9 1.7 all_gather_reshape.3
  24.7 0.8 reshape.297
  25.9 0.8 broadcast_select_fusion
  26.6 0.7 fusion.25.x_ref
  27.3 50.0 %shard_map.46 = bf16[16,17,2432]{2,1,0:T(8,128)(2,1)} custom-call(bf16[17,2432]{1,0:T(8,128)(2,1)} %fusion.25.x_ref), custom_call_target="tpu_custom_call" | custom-call | tf_op jit(solution)/shard_map/pallas_call | solution.py:45
  77.3 2.7 copy.41
  80.1 3.1 %copy.42 = bf16[10,4,4,4,2432]{4,3,2,1,0:T(4,128)(2,1)S(1)} copy(bf16[10,4,4,4,2432]{4,3,0,1,2:T(4,128)(2,1)} %bitcast.47) | data formatting | bytes 6225920 | tf_op jit(solution)/shard_map/transpose | solution.py:198
  83.3 3.5 %reshape.298 = bf16[640,2432]{1,0:T(8,128)(2,1)} reshape(bf16[10,4,4,4,2432]{4,3,2,1,0:T(4,128)(2,1)S(1)} %copy.42) | data formatting | bytes 6225920 | tf_op jit(solution)/shard_map/reshape | solution.py:198
  86.8 54.4 %all-gather.11.cloned.1.call-done = bf16[64,17,2432]{2,0,1:T(8,128)(2,1)} async-done(((bf16[16,17,2432]{2,0,1:T(8,128)(2,1)}), bf16[64,17,2432]{2,0,1:T(8,128)(2,1)}) %all-gather.11.cloned.1.call-update) | async-done | bytes 5292048 | tf_op jit(solution)/shard_map/all_gather | solution.py:197
  141.2 1.7 constant_dynamic-slice_fusion.1
  143.8 2.8 slice.91
  146.6 6.2 %copy.45 = bf16[4,4,16,4,2432]{4,3,2,1,0:T(4,128)(2,1)} copy(bf16[4,4,16,4,2432]{4,2,1,3,0:T(8,128)(2,1)S(1)} %bitcast.43) | data formatting | bytes 9961472 | tf_op jit(solution)/shard_map/transpose | solution.py:205
  152.7 8.8 %reshape.301 = bf16[1024,2432]{1,0:T(8,128)(2,1)} reshape(bf16[4,4,16,4,2432]{4,3,2,1,0:T(4,128)(2,1)} %copy.45) | data formatting | bytes 9961472 | tf_op jit(solution)/shard_map/reshape | solution.py:205
  161.5 0.7 slice_convert_fusion
  162.7 10.9 %select_add_fusion.a_ref = f32[1024,1024]{1,0:T(8,128)} fusion(f32[1024]{0:T(1024)S(1)} %broadcast_in_dim.78, bf16[1024,2432]{1,0:T(8,128)(2,1)} %reshape.301), kind=kOutput, calls=%fused_computation.8 | convolution fusion | flops 5103419392 | bytes 9179136 | tf_op jit(solution)/shard_map/dot_general | solution.py:229
  173.7 79.0 %shard_map.47 = f32[1024,1024]{1,0:T(8,128)S(1)} custom-call(f32[1024,1024]{1,0:T(8,128)} %select_add_fusion.a_ref), custom_call_target="tpu_custom_call" | custom-call | flops 2147483648 | bytes 8388608 | tf_op jit(solution)/shard_map/pallas_call | solution.py:132
  252.7 1.9 copy-done.2
  254.7 3.1 %copy.43 = bf16[10,16,4,2432]{3,2,1,0:T(4,128)(2,1)S(1)} copy(bf16[10,16,4,2432]{3,2,0,1:T(4,128)(2,1)} %bitcast.46) | data formatting | bytes 6225920 | tf_op jit(solution)/shard_map/transpose | solution.py:209
  257.8 3.0 reshape.299
  260.8 6.8 %fusion.39 = f32[640,640]{0,1:T(8,128)} fusion(bf16[640,2432]{1,0:T(8,128)(2,1)} %reshape.299, bf16[640,2432]{1,0:T(8,128)(2,1)} %reshape.298), kind=kOutput, calls=%fused_computation.76 | convolution fusion | flops 1992294400 | bytes 7864320 | tf_op jit(solution)/shard_map/dot_general | solution.py:239
  267.7 10.7 %fusion = f32[1280,1024]{1,0:T(8,128)S(1)} fusion(bf16[1024,2432]{1,0:T(8,128)(2,1)} %reshape.301, bf16[640,2432]{1,0:T(8,128)(2,1)S(1)} %copy-done.5, bf16[640,2432]{1,0:T(8,128)(2,1)S(1)} %copy-done.6), kind=kOutput, calls=%fused_computation | convolution fusion | flops 6387793920 | bytes 16449536 | tf_op jit(solution)/shard_map/dot_general | solution.py:235
  278.4 8.9 %fusion.4 = f32[1280,1024]{1,0:T(8,128)S(1)} fusion(f32[1024,1024]{1,0:T(8,128)S(1)} %copy-done.3, f32[1280,1024]{1,0:T(8,128)S(1)} %fusion, f32[1024]{0:T(1024)S(1)} %broadcast_in_dim.78, s32[1280]{0:T(1024)S(1)} %pad_add_fusion), kind=kOutput, calls=%fused_computation.4 | convolution fusion | flops 8056995840 | bytes 14689280 | tf_op jit(solution)/shard_map/dot_general | solution.py:245
  287.3 2.3 copy-done.4
  289.8 2.3 copy.48
  292.1 1.0 constant_dynamic-slice_fusion
  293.3 5.9 %fusion.13 = f32[640,576]{0,1:T(8,128)S(1)} fusion(f32[640,640]{0,1:T(8,128)} %fusion.39, f32[1280,1024]{1,0:T(8,128)} %copy-done.4, f32[576]{0:T(1024)S(1)} %slice.112, s32[640]{0:T(1024)S(1)} %add.143, s32[576]{0:T(1024)S(1)} %slice.111, pred[640]{0:T(1024)(128)(4,1)S(1)} %broadcast_compare_fusion), kind=kOutput, calls=%fused_computation.18 | convolution fusion | flops 2266767360 | bytes 7937664 | tf_op jit(solution)/shard_map/dot_general | solution.py:260
  299.3 1.7 copy.49
  (64 shorter events, 3.9 us)
Async XLA Ops:
  6.5 2.1 copy-start
  6.5 70.8 %all-gather.7.cloned.1.call-start = ((), (), s32[]{:S(2)}) async-start(), calls=%async_computation | async-start | bytes 3891200 | tf_op jit(solution)/shard_map/all_gather | solution.py:194
  24.6 116.6 %all-gather.11.cloned.1.call-start = ((), (), s32[]{:S(2)}) async-start(), calls=%async_computation.2 | async-start | bytes 6615040 | tf_op jit(solution)/shard_map/all_gather | solution.py:197
  25.4 54.7 %copy-start.7 = (bf16[4,10,4,2432]{3,2,1,0:T(4,128)(2,1)}, bf16[4,10,4,2432]{3,2,1,0:T(4,128)(2,1)S(1)}, u32[]{:S(2)}) copy-start(bf16[4,10,4,2432]{3,2,1,0:T(4,128)(2,1)S(1)} %reshape.297) | copy-start | bytes 2334724
  80.1 174.6 %all-gather.9.cloned.1.call-start = ((), (), s32[]{:S(2)}) async-start(), calls=%async_computation.1 | async-start | bytes 3307520 | tf_op jit(solution)/shard_map/all_gather | solution.py:208
  83.3 59.6 %copy-start.8 = (f32[40]{0:T(128)S(1)}, f32[40]{0:T(128)}, u32[]{:S(2)}) copy-start(f32[40]{0:T(128)} %param.11) | copy-start | bytes 484
  252.7 1.9 copy-start.2
  260.8 6.8 %copy-start.5 = (bf16[640,2432]{1,0:T(8,128)(2,1)S(1)}, bf16[640,2432]{1,0:T(8,128)(2,1)}, u32[]{:S(2)}) copy-start(bf16[640,2432]{1,0:T(8,128)(2,1)} %reshape.298) | copy-start | bytes 9338884
  260.8 6.8 %copy-start.6 = (bf16[640,2432]{1,0:T(8,128)(2,1)S(1)}, bf16[640,2432]{1,0:T(8,128)(2,1)}, u32[]{:S(2)}) copy-start(bf16[640,2432]{1,0:T(8,128)(2,1)} %reshape.299) | copy-start | bytes 9338884
  267.7 10.7 %copy-start.3 = (f32[1024,1024]{1,0:T(8,128)S(1)}, f32[1024,1024]{1,0:T(8,128)}, u32[]{:S(2)}) copy-start(f32[1024,1024]{1,0:T(8,128)} %copy-done.2) | copy-start | bytes 12582916
  287.3 2.3 copy-start.4
  293.3 7.8 %copy-start.1 = (bf16[2,304,160]{1,2,0:T(8,128)(2,1)S(1)}, bf16[2,304,160]{1,2,0:T(8,128)(2,1)}, u32[]{:S(2)}) copy-start(bf16[2,304,160]{1,2,0:T(8,128)(2,1)} %param.8) | copy-start | bytes 583684
Sparse Core Ops, SparseCore 0:
  24.7 43.8 all-gather.6
  80.2 60.9 all-gather.10
  143.8 90.2 all-gather.8

commit v4 on v3

--- a/solution.py
+++ b/solution.py
@@ -194,15 +194,27 @@
     col_w = lax.all_gather(every, "row", axis=0, tiled=False)
     panel_w = remote_gather(panel_w, "col", colcount, 0)
     panel_w, col_w = lax.optimization_barrier((panel_w, col_w))
-    panel_w = lax.all_gather(panel_w, "row", axis=0, tiled=False)
+    split = 10 * 128
+    first_half = lax.all_gather(panel_w[:, :, :split], "row", axis=0, tiled=False)
+    second_half = lax.all_gather(panel_w[:, :, split:], "row", axis=0, tiled=False)
     col_w = jnp.transpose(col_w, (2, 1, 0, 3, 4)).reshape(NPAN * owners * window, total)
-    every, panel_w, col_w = lax.optimization_barrier((every, panel_w, col_w))
-    shift_panel = join3(panel_w[:, :, groups * window, : 3 * groups * window])
+    shift_panel = join3(first_half[:, :, groups * window, : 3 * groups * window])
     shift_panel = jnp.transpose(
         shift_panel.reshape(rowcount, colcount, groups, window), (2, 0, 1, 3)
     ).reshape(PW)
-    panel_w = panel_w[:, :, : groups * window].reshape(rowcount, colcount, groups, window, total)
-    panel_w = jnp.transpose(panel_w, (2, 0, 1, 3, 4)).reshape(PW, total)
+
+    def natural(half):
+        half = half[:, :, : groups * window].reshape(
+            rowcount, colcount, groups, window, half.shape[-1]
+        )
+        return jnp.transpose(half, (2, 0, 1, 3, 4)).reshape(PW, half.shape[-1])
+
+    first_half = natural(first_half)
+    dims_half = (((1,), (1,)), ((), ()))
+    first_block = lax.dot_general(first_half, first_half, dims_half, preferred_element_type=jnp.float32)
+    every, second_half, col_w = lax.optimization_barrier((every, second_half, col_w))
+    second_half = natural(second_half)
+    panel_w = jnp.concatenate([first_half, second_half], axis=1)
 
     row_w = lax.dynamic_index_in_dim(every, group_index, 0, keepdims=False)
     row_w = lax.all_gather(row_w, "col", axis=0, tiled=False)
@@ -226,7 +238,9 @@
 
     dims = (((1,), (1,)), ((), ()))
     f32 = jnp.float32
-    diag_block = lax.dot_general(panel_w, panel_w, dims, preferred_element_type=f32)
+    diag_block = first_block + lax.dot_general(
+        second_half, second_half, dims, preferred_element_type=f32
+    )
     diag_block = diag_block + jnp.where(
         panel_ids_all[:, None] == panel_ids_all[None, :], shift_panel[None, :], 0.0
     )

time: 313 us -> 313 us (level)
  waiting for transfers between devices: 54.5 us -> 63.2 us
  local copies, waits for them, and re-layouts: 49.1 us -> 43.6 us
  matrix products: 45.4 us -> 41.4 us
    all_gather x1 -> x2, waiting for transfers between devices: 54.4 us -> 63.1 us  [the longest x1 32.7 us: local(): lax.all_gather(panel_w[:, :, :split], 'row', axis=0, tiled=False)]
    reshape x1 -> x2, local copies, waits for them, and re-layouts: 8.75 us -> 4.39 us  [natural(): return jnp.transpose(half, (2, 0, 1, 3, 4)).reshape(PW, half.shape[-1])]
    slice x1 -> x7, local copies, waits for them, and re-layouts: 2.76 us -> 6.95 us  [the longest x2 3.76 us: natural(): half[:, :, :groups * window]]
    dot_general x1, matrix products: 10.7 us -> 6.98 us  [local(): lax.dot_general(both_w, panel_w, dims, preferred_element_type=f32)]
    dot_general x1 -> x2, matrix products: 10.9 us -> 10.4 us  [the longest x1 5.58 us: local(): lax.dot_general(first_half, first_half, dims_half, preferred_element_type...]
  transfers between devices with their start and end apart: 3 -> 4, of which waited for: 1 -> 2; matrix products, arithmetic and copies ran while one was open for 13% -> 12% of each run, Pallas kernels for 42% -> 42%
where the time goes in v4:
time: 313 us; the launch traced here: 308 us
  Pallas kernels  129 us (41%)
  waiting for transfers between devices  63.2 us (20%)
  local copies, waits for them, and re-layouts  43.6 us (14%)
  matrix products  41.4 us (13%)
  between operations  13.8 us (4%)
  blocking collectives  10.5 us (3%)
  other arithmetic  5.46 us (2%)
    pallas_call x1, Pallas kernels, inverse_cholesky(): pl.pallas_call(functools.partial(_kernel, n=n, b=b), out_shape=jax.ShapeD...  79.4 us
    pallas_call x1, Pallas kernels, remote_gather(): pl.pallas_call(functools.partial(_gather_kernel, axis=axis, count=count),...  50 us
    all_gather x1, waiting for transfers between devices, local(): lax.all_gather(panel_w[:, :, :split], 'row', axis=0, tiled=False)  32.7 us
    all_gather x1, waiting for transfers between devices, local(): lax.all_gather(panel_w[:, :, split:], 'row', axis=0, tiled=False)  30.5 us
    all_gather x1, blocking collectives, local(): lax.all_gather(jnp.concatenate([whitened, shift_row], axis=0), 'grp', axi...  10.5 us
    dot_general x1, matrix products, local(): lax.dot_general(both_panel, inverse_factor_panel, dims, precision=high, p...  9.19 us
    dot_general x1, matrix products, local(): lax.dot_general(both_w, panel_w, dims, preferred_element_type=f32)  6.98 us
    dot_general x1, matrix products, local(): schur_tile = lax.dot_general(row_w, col_w, dims, preferred_element_type=f32)  6.82 us
  transfers between devices with their start and end apart: 4, of which 2 were waited for; matrix products, arithmetic and copies ran while one was open for 12% of the time, Pallas kernels for 42%

profile of v4, /device:TPU:1, one launch (start us, length us, event | category | flops | bytes accessed | tf_op | source)
XLA Modules:
  0.0 307.5 jit_solution(1588054357692387498)
XLA Ops:
  8.6 2.1 fusion.19
  11.8 10.5 %all-gather.3 = bf16[4,161,608]{2,1,0:T(8,128)(2,1)S(1)} all-gather(bf16[1,161,608]{2,1,0:T(8,128)(2,1)S(1)} %fusion.27), channel_id=2, replica_groups=mesh['grp'=4,'row'=4,'col'=16] {'grp'}, dimensions={0}, use_global_device_ids=true | all-gather | bytes 978880 | tf_op jit(solution)/shard_map/all_gather | solution.py:184
  22.9 1.7 all_gather_reshape.3
  27.2 50.0 %shard_map.46 = bf16[16,17,2432]{2,1,0:T(8,128)(2,1)} custom-call(bf16[17,2432]{1,0:T(8,128)(2,1)} %fusion.28.x_ref), custom_call_target="tpu_custom_call" | custom-call | tf_op jit(solution)/shard_map/pallas_call | solution.py:45
  77.3 1.3 slice.100
  78.6 0.9 copy.45
  79.6 1.0 copy.48
  80.7 3.1 %copy.46 = bf16[10,4,4,4,2432]{4,3,2,1,0:T(4,128)(2,1)S(1)} copy(bf16[10,4,4,4,2432]{4,3,0,1,2:T(4,128)(2,1)} %bitcast.51) | data formatting | bytes 6225920 | tf_op jit(solution)/shard_map/transpose | solution.py:200
  83.8 3.3 %reshape.304 = bf16[640,2432]{1,0:T(8,128)(2,1)} reshape(bf16[10,4,4,4,2432]{4,3,2,1,0:T(4,128)(2,1)S(1)} %copy.46) | data formatting | bytes 6225920 | tf_op jit(solution)/shard_map/reshape | solution.py:200
  87.1 30.5 %all-gather.13.cloned.1.call-done = bf16[64,17,1152]{2,0,1:T(8,128)(2,1)} async-done(((bf16[16,17,1152]{2,0,1:T(8,128)(2,1)}), bf16[64,17,1152]{2,0,1:T(8,128)(2,1)}) %all-gather.13.cloned.1.call-update) | async-done | bytes 2506768 | tf_op jit(solution)/shard_map/all_gather | solution.py:199
  117.5 1.7 constant_dynamic-slice_fusion.1
  120.2 1.8 slice.103
  122.0 1.8 copy.52
  123.8 2.2 reshape.309
  126.0 32.7 %all-gather.15.cloned.1.call-done = bf16[64,17,1280]{2,0,1:T(8,128)(2,1)} async-done(((bf16[16,17,1280]{2,0,1:T(8,128)(2,1)}), bf16[64,17,1280]{2,0,1:T(8,128)(2,1)}) %all-gather.15.cloned.1.call-update) | async-done | bytes 2785296 | tf_op jit(solution)/shard_map/all_gather | solution.py:198
  158.6 1.9 slice.119
  160.6 2.0 copy.50
  162.6 2.2 reshape.307
  166.1 5.6 %fusion.42 = f32[1024,1024]{1,0:T(8,128)S(1)} fusion(bf16[1024,1280]{1,0:T(8,128)(2,1)} %reshape.307), kind=kOutput, calls=%fused_computation.79 | convolution fusion | flops 2684354560 | bytes 6815744 | tf_op jit(solution)/shard_map/dot_general | solution.py:214
  171.7 4.9 %select_add_fusion.a_ref = f32[1024,1024]{1,0:T(8,128)} fusion(f32[1024,1024]{1,0:T(8,128)S(1)} %fusion.42, f32[1024]{0:T(1024)S(1)} %broadcast_in_dim.78, bf16[1024,1152]{1,0:T(8,128)(2,1)S(1)} %copy-done.8), kind=kOutput, calls=%fused_computation.11 | convolution fusion | flops 2420113408 | bytes 10752000 | tf_op jit(solution)/shard_map/dot_general | solution.py:241
  176.6 79.4 %shard_map.47 = f32[1024,1024]{1,0:T(8,128)S(1)} custom-call(f32[1024,1024]{1,0:T(8,128)} %select_add_fusion.a_ref), custom_call_target="tpu_custom_call" | custom-call | flops 2147483648 | bytes 8388608 | tf_op jit(solution)/shard_map/pallas_call | solution.py:132
  255.9 1.9 copy-done.2
  257.9 3.1 %copy.47 = bf16[10,16,4,2432]{3,2,1,0:T(4,128)(2,1)S(1)} copy(bf16[10,16,4,2432]{3,2,0,1:T(4,128)(2,1)} %bitcast.50) | data formatting | bytes 6225920 | tf_op jit(solution)/shard_map/transpose | solution.py:221
  261.0 3.2 %reshape.305 = bf16[640,2432]{1,0:T(8,128)(2,1)} reshape(bf16[10,16,4,2432]{3,2,1,0:T(4,128)(2,1)S(1)} %copy.47) | data formatting | bytes 6225920 | tf_op jit(solution)/shard_map/reshape | solution.py:221
  264.2 6.8 %fusion.43 = f32[640,640]{0,1:T(8,128)} fusion(bf16[640,2432]{1,0:T(8,128)(2,1)} %reshape.305, bf16[640,2432]{1,0:T(8,128)(2,1)} %reshape.304), kind=kOutput, calls=%fused_computation.80 | convolution fusion | flops 1992294400 | bytes 7864320 | tf_op jit(solution)/shard_map/dot_general | solution.py:253
  271.1 7.0 %fusion = f32[1280,1024]{1,0:T(8,128)S(1)} fusion(bf16[640,2432]{1,0:T(8,128)(2,1)S(1)} %copy-done.5, bf16[640,2432]{1,0:T(8,128)(2,1)S(1)} %copy-done.6, bf16[1024,1152]{1,0:T(8,128)(2,1)S(1)} %copy-done.9, bf16[1024,1280]{1,0:T(8,128)(2,1)S(1)} %copy-done.7), kind=kOutput, calls=%fused_computation | convolution fusion | flops 6397755392 | bytes 16449536 | tf_op jit(solution)/shard_map/dot_general | solution.py:249
  278.1 9.2 %fusion.4 = f32[1280,1024]{1,0:T(8,128)S(1)} fusion(f32[1024,1024]{1,0:T(8,128)S(1)} %copy-done.3, f32[1280,1024]{1,0:T(8,128)S(1)} %fusion, f32[1024]{0:T(1024)S(1)} %broadcast_in_dim.78, s32[1280]{0:T(1024)S(1)} %pad_add_fusion), kind=kOutput, calls=%fused_computation.4 | convolution fusion | flops 8056995840 | bytes 14689280 | tf_op jit(solution)/shard_map/dot_general | solution.py:259
  287.3 2.3 copy-done.4
  289.8 2.1 copy.55
  291.9 1.0 constant_dynamic-slice_fusion
  293.0 5.9 %fusion.16 = f32[640,576]{0,1:T(8,128)S(1)} fusion(f32[640,640]{0,1:T(8,128)} %fusion.43, f32[1280,1024]{1,0:T(8,128)} %copy-done.4, f32[576]{0:T(1024)S(1)} %slice.126, s32[640]{0:T(1024)S(1)} %add.146, s32[576]{0:T(1024)S(1)} %slice.125, pred[640]{0:T(1024)(128)(4,1)S(1)} %broadcast_compare_fusion), kind=kOutput, calls=%fused_computation.21 | convolution fusion | flops 2266767360 | bytes 7937664 | tf_op jit(solution)/shard_map/dot_general | solution.py:274
  299.1 1.7 copy.56
  (81 shorter events, 9.0 us)
Async XLA Ops:
  6.5 2.1 copy-start
  6.5 70.8 %all-gather.9.cloned.1.call-start = ((), (), s32[]{:S(2)}) async-start(), calls=%async_computation | async-start | bytes 3891200 | tf_op jit(solution)/shard_map/all_gather | solution.py:194
  24.6 93.0 %all-gather.13.cloned.1.call-start = ((), (), s32[]{:S(2)}) async-start(), calls=%async_computation.2 | async-start | bytes 3133440 | tf_op jit(solution)/shard_map/all_gather | solution.py:199
  25.4 54.1 %copy-start.10 = (bf16[4,10,4,2432]{3,2,1,0:T(4,128)(2,1)}, bf16[4,10,4,2432]{3,2,1,0:T(4,128)(2,1)S(1)}, u32[]{:S(2)}) copy-start(bf16[4,10,4,2432]{3,2,1,0:T(4,128)(2,1)S(1)} %reshape.303) | copy-start | bytes 2334724
  77.3 2.3 slice-start
  79.6 79.1 %all-gather.15.cloned.1.call-start = ((), (), s32[]{:S(2)}) async-start(), calls=%async_computation.3 | async-start | bytes 3481600 | tf_op jit(solution)/shard_map/all_gather | solution.py:198
  80.6 177.2 %all-gather.11.cloned.1.call-start = ((), (), s32[]{:S(2)}) async-start(), calls=%async_computation.1 | async-start | bytes 3307520 | tf_op jit(solution)/shard_map/all_gather | solution.py:220
  83.8 35.4 %copy-start.11 = (f32[40]{0:T(128)S(1)}, f32[40]{0:T(128)}, u32[]{:S(2)}) copy-start(f32[40]{0:T(128)} %param.11) | copy-start | bytes 484
  166.1 5.6 %copy-start.8 = (bf16[1024,1152]{1,0:T(8,128)(2,1)S(1)}, bf16[1024,1152]{1,0:T(8,128)(2,1)}, u32[]{:S(2)}) copy-start(bf16[1024,1152]{1,0:T(8,128)(2,1)} %reshape.309) | copy-start | bytes 7077892
  255.9 1.9 copy-start.2
  264.2 6.9 %copy-start.5 = (bf16[640,2432]{1,0:T(8,128)(2,1)S(1)}, bf16[640,2432]{1,0:T(8,128)(2,1)}, u32[]{:S(2)}) copy-start(bf16[640,2432]{1,0:T(8,128)(2,1)} %reshape.304) | copy-start | bytes 9338884
  264.2 6.9 %copy-start.6 = (bf16[640,2432]{1,0:T(8,128)(2,1)S(1)}, bf16[640,2432]{1,0:T(8,128)(2,1)}, u32[]{:S(2)}) copy-start(bf16[640,2432]{1,0:T(8,128)(2,1)} %reshape.305) | copy-start | bytes 9338884
  264.2 6.9 %copy-start.7 = (bf16[1024,1280]{1,0:T(8,128)(2,1)S(1)}, bf16[1024,1280]{1,0:T(8,128)(2,1)}, u32[]{:S(2)}) copy-start(bf16[1024,1280]{1,0:T(8,128)(2,1)} %reshape.307) | copy-start | bytes 7864324
  264.2 6.8 %copy-start.9 = (bf16[1024,1152]{1,0:T(8,128)(2,1)S(1)}, bf16[1024,1152]{1,0:T(8,128)(2,1)}, u32[]{:S(2)}) copy-start(bf16[1024,1152]{1,0:T(8,128)(2,1)} %reshape.309) | copy-start | bytes 7077892
  271.1 7.0 %copy-start.3 = (f32[1024,1024]{1,0:T(8,128)S(1)}, f32[1024,1024]{1,0:T(8,128)}, u32[]{:S(2)}) copy-start(f32[1024,1024]{1,0:T(8,128)} %copy-done.2) | copy-start | bytes 12582916
  287.3 2.3 copy-start.4
  293.0 7.7 %copy-start.1 = (bf16[2,304,160]{1,2,0:T(8,128)(2,1)S(1)}, bf16[2,304,160]{1,2,0:T(8,128)(2,1)}, u32[]{:S(2)}) copy-start(bf16[2,304,160]{1,2,0:T(8,128)(2,1)} %param.8) | copy-start | bytes 583684
Sparse Core Ops, SparseCore 0:
  24.7 43.8 all-gather.8
  79.7 37.8 all-gather.12
  119.4 39.2 all-gather.14
  161.1 89.7 all-gather.10

commit v5 on v4

--- a/solution.py
+++ b/solution.py
@@ -181,9 +181,7 @@
     shift_row = jnp.zeros((1, stacked), jnp.bfloat16).at[0, : 3 * shift.shape[0]].set(
         split3(shift)
     )
-    every = lax.all_gather(
-        jnp.concatenate([whitened, shift_row], axis=0), "grp", axis=0, tiled=False
-    )
+    every = remote_gather(jnp.concatenate([whitened, shift_row], axis=0), "grp", groups, 2)
     shift_grp = join3(every[:, local_cols, : 3 * shift.shape[0]]).reshape(groups, NPAN, window)
     every = jnp.transpose(every[:, :local_cols], (1, 0, 2)).reshape(groups, NPAN, window, total)
 

time: 313 us -> 319 us (1.019)
  Pallas kernels: 129 us -> 144 us
  blocking collectives: 10.5 us -> 0 us
    pallas_call x1 -> x2, Pallas kernels: 50 us -> 64.2 us  [remote_gather(): pl.pallas_call(functools.partial(_gather_kernel, axis=axis, count=count),...]
    all_gather x1 -> x0, blocking collectives: 10.5 us -> none  [local(): lax.all_gather(jnp.concatenate([whitened, shift_row], axis=0), 'grp', axi...]
  transfers between devices with their start and end apart: 4 -> 4, of which waited for: 2 -> 2; matrix products, arithmetic and copies ran while one was open for 12% -> 12% of each run, Pallas kernels for 42% -> 41%
where the time goes in v5:
time: 319 us; the launch traced here: 314 us
  Pallas kernels  144 us (45%)
  waiting for transfers between devices  63.3 us (20%)
  local copies, waits for them, and re-layouts  44.8 us (14%)
  matrix products  41.4 us (13%)
  between operations  13.8 us (4%)
  other arithmetic  6.97 us (2%)
    pallas_call x1, Pallas kernels, inverse_cholesky(): pl.pallas_call(functools.partial(_kernel, n=n, b=b), out_shape=jax.ShapeD...  79.4 us
    pallas_call x2, Pallas kernels, remote_gather(): pl.pallas_call(functools.partial(_gather_kernel, axis=axis, count=count),...  64.2 us
    all_gather x1, waiting for transfers between devices, local(): lax.all_gather(panel_w[:, :, :split], 'row', axis=0, tiled=False)  32.7 us
    all_gather x1, waiting for transfers between devices, local(): lax.all_gather(panel_w[:, :, split:], 'row', axis=0, tiled=False)  30.6 us
    dot_general x1, matrix products, local(): lax.dot_general(both_panel, inverse_factor_panel, dims, precision=high, p...  9.19 us
    dot_general x1, matrix products, local(): lax.dot_general(both_w, panel_w, dims, preferred_element_type=f32)  6.98 us
    dot_general x1, matrix products, local(): schur_tile = lax.dot_general(row_w, col_w, dims, preferred_element_type=f32)  6.82 us
  transfers between devices with their start and end apart: 4, of which 2 were waited for; matrix products, arithmetic and copies ran while one was open for 12% of the time, Pallas kernels for 41%

profile of v5, /device:TPU:1, one launch (start us, length us, event | category | flops | bytes accessed | tf_op | source)
XLA Modules:
  0.0 314.0 jit_solution(1643019405653820386)
XLA Ops:
  8.6 2.1 fusion.19
  12.6 15.2 %shard_map.46 = bf16[4,161,608]{2,1,0:T(8,128)(2,1)} custom-call(bf16[161,608]{1,0:T(8,128)(2,1)} %fusion.26.x_ref), custom_call_target="tpu_custom_call" | custom-call | tf_op jit(solution)/shard_map/pallas_call | solution.py:45
  27.8 1.2 slice_bitcast_fusion
  29.4 1.7 all_gather_reshape.3
  34.6 49.1 %shard_map.47 = bf16[16,17,2432]{2,1,0:T(8,128)(2,1)} custom-call(bf16[17,2432]{1,0:T(8,128)(2,1)} %fusion.27.x_ref), custom_call_target="tpu_custom_call" | custom-call | tf_op jit(solution)/shard_map/pallas_call | solution.py:45
  83.7 1.3 slice.100
  86.0 1.0 copy.49
  87.0 3.1 copy.47
  90.2 3.3 %reshape.304 = bf16[640,2432]{1,0:T(8,128)(2,1)} reshape(bf16[10,4,4,4,2432]{4,3,2,1,0:T(4,128)(2,1)S(1)} %copy.47) | data formatting | bytes 6225920 | tf_op jit(solution)/shard_map/reshape | solution.py:198
  93.4 30.6 %all-gather.11.cloned.1.call-done = bf16[64,17,1152]{2,0,1:T(8,128)(2,1)} async-done(((bf16[16,17,1152]{2,0,1:T(8,128)(2,1)}), bf16[64,17,1152]{2,0,1:T(8,128)(2,1)}) %all-gather.11.cloned.1.call-update) | async-done | bytes 2506768 | tf_op jit(solution)/shard_map/all_gather | solution.py:197
  124.0 1.7 constant_dynamic-slice_fusion.1
  126.6 1.8 slice.103
  128.5 1.8 copy.53
  130.3 2.2 reshape.309
  132.4 32.7 %all-gather.13.cloned.1.call-done = bf16[64,17,1280]{2,0,1:T(8,128)(2,1)} async-done(((bf16[16,17,1280]{2,0,1:T(8,128)(2,1)}), bf16[64,17,1280]{2,0,1:T(8,128)(2,1)}) %all-gather.13.cloned.1.call-update) | async-done | bytes 2785296 | tf_op jit(solution)/shard_map/all_gather | solution.py:196
  165.1 1.9 slice.117
  167.0 2.0 copy.51
  169.0 2.2 reshape.307
  172.6 5.6 %fusion.40 = f32[1024,1024]{1,0:T(8,128)S(1)} fusion(bf16[1024,1280]{1,0:T(8,128)(2,1)} %reshape.307), kind=kOutput, calls=%fused_computation.77 | convolution fusion | flops 2684354560 | bytes 6815744 | tf_op jit(solution)/shard_map/dot_general | solution.py:212
  178.1 4.9 %select_add_fusion.a_ref = f32[1024,1024]{1,0:T(8,128)} fusion(f32[1024,1024]{1,0:T(8,128)S(1)} %fusion.40, f32[1024]{0:T(1024)S(1)} %broadcast_in_dim.78, bf16[1024,1152]{1,0:T(8,128)(2,1)S(1)} %copy-done.8), kind=kOutput, calls=%fused_computation.11 | convolution fusion | flops 2420113408 | bytes 10752000 | tf_op jit(solution)/shard_map/dot_general | solution.py:239
  183.0 79.4 %shard_map.48 = f32[1024,1024]{1,0:T(8,128)S(1)} custom-call(f32[1024,1024]{1,0:T(8,128)} %select_add_fusion.a_ref), custom_call_target="tpu_custom_call" | custom-call | flops 2147483648 | bytes 8388608 | tf_op jit(solution)/shard_map/pallas_call | solution.py:132
  262.4 1.9 copy-done.2
  264.3 3.1 copy.48
  267.5 3.2 %reshape.305 = bf16[640,2432]{1,0:T(8,128)(2,1)} reshape(bf16[10,16,4,2432]{3,2,1,0:T(4,128)(2,1)S(1)} %copy.48) | data formatting | bytes 6225920 | tf_op jit(solution)/shard_map/reshape | solution.py:219
  270.7 6.8 %fusion.41 = f32[640,640]{0,1:T(8,128)} fusion(bf16[640,2432]{1,0:T(8,128)(2,1)} %reshape.305, bf16[640,2432]{1,0:T(8,128)(2,1)} %reshape.304), kind=kOutput, calls=%fused_computation.78 | convolution fusion | flops 1992294400 | bytes 7864320 | tf_op jit(solution)/shard_map/dot_general | solution.py:251
  277.5 7.0 %fusion = f32[1280,1024]{1,0:T(8,128)S(1)} fusion(bf16[640,2432]{1,0:T(8,128)(2,1)S(1)} %copy-done.5, bf16[640,2432]{1,0:T(8,128)(2,1)S(1)} %copy-done.6, bf16[1024,1152]{1,0:T(8,128)(2,1)S(1)} %copy-done.9, bf16[1024,1280]{1,0:T(8,128)(2,1)S(1)} %copy-done.7), kind=kOutput, calls=%fused_computation | convolution fusion | flops 6397755392 | bytes 16449536 | tf_op jit(solution)/shard_map/dot_general | solution.py:247
  284.5 9.2 %fusion.4 = f32[1280,1024]{1,0:T(8,128)S(1)} fusion(f32[1024,1024]{1,0:T(8,128)S(1)} %copy-done.3, f32[1280,1024]{1,0:T(8,128)S(1)} %fusion, f32[1024]{0:T(1024)S(1)} %broadcast_in_dim.78, s32[1280]{0:T(1024)S(1)} %pad_add_fusion), kind=kOutput, calls=%fused_computation.4 | convolution fusion | flops 8056995840 | bytes 14689280 | tf_op jit(solution)/shard_map/dot_general | solution.py:257
  293.7 2.3 copy-done.4
  296.2 2.1 copy.56
  298.3 1.0 constant_dynamic-slice_fusion
  299.5 5.9 %fusion.16 = f32[640,576]{0,1:T(8,128)S(1)} fusion(f32[640,640]{0,1:T(8,128)} %fusion.41, f32[1280,1024]{1,0:T(8,128)} %copy-done.4, f32[576]{0:T(1024)S(1)} %slice.124, s32[640]{0:T(1024)S(1)} %add.146, s32[576]{0:T(1024)S(1)} %slice.123, pred[640]{0:T(1024)(128)(4,1)S(1)} %broadcast_compare_fusion), kind=kOutput, calls=%fused_computation.21 | convolution fusion | flops 2266767360 | bytes 7937664 | tf_op jit(solution)/shard_map/dot_general | solution.py:272
  305.5 1.7 copy.57
  (81 shorter events, 11.4 us)
Async XLA Ops:
  6.5 2.1 copy-start
  6.5 77.1 %all-gather.7.cloned.1.call-start = ((), (), s32[]{:S(2)}) async-start(), calls=%async_computation | async-start | bytes 3891200 | tf_op jit(solution)/shard_map/all_gather | solution.py:192
  31.1 92.8 %all-gather.11.cloned.1.call-start = ((), (), s32[]{:S(2)}) async-start(), calls=%async_computation.2 | async-start | bytes 3133440 | tf_op jit(solution)/shard_map/all_gather | solution.py:197
  32.0 2.6 copy-start.10
  83.6 2.3 slice-start
  85.9 79.2 %all-gather.13.cloned.1.call-start = ((), (), s32[]{:S(2)}) async-start(), calls=%async_computation.3 | async-start | bytes 3481600 | tf_op jit(solution)/shard_map/all_gather | solution.py:196
  87.0 177.3 %all-gather.9.cloned.1.call-start = ((), (), s32[]{:S(2)}) async-start(), calls=%async_computation.1 | async-start | bytes 3307520 | tf_op jit(solution)/shard_map/all_gather | solution.py:218
  90.2 35.5 %copy-start.11 = (f32[40]{0:T(128)S(1)}, f32[40]{0:T(128)}, u32[]{:S(2)}) copy-start(f32[40]{0:T(128)} %param.11) | copy-start | bytes 484
  172.5 5.6 %copy-start.8 = (bf16[1024,1152]{1,0:T(8,128)(2,1)S(1)}, bf16[1024,1152]{1,0:T(8,128)(2,1)}, u32[]{:S(2)}) copy-start(bf16[1024,1152]{1,0:T(8,128)(2,1)} %reshape.309) | copy-start | bytes 7077892
  262.4 1.9 copy-start.2
  270.6 6.9 %copy-start.5 = (bf16[640,2432]{1,0:T(8,128)(2,1)S(1)}, bf16[640,2432]{1,0:T(8,128)(2,1)}, u32[]{:S(2)}) copy-start(bf16[640,2432]{1,0:T(8,128)(2,1)} %reshape.304) | copy-start | bytes 9338884
  270.7 6.9 %copy-start.6 = (bf16[640,2432]{1,0:T(8,128)(2,1)S(1)}, bf16[640,2432]{1,0:T(8,128)(2,1)}, u32[]{:S(2)}) copy-start(bf16[640,2432]{1,0:T(8,128)(2,1)} %reshape.305) | copy-start | bytes 9338884
  270.7 6.9 %copy-start.7 = (bf16[1024,1280]{1,0:T(8,128)(2,1)S(1)}, bf16[1024,1280]{1,0:T(8,128)(2,1)}, u32[]{:S(2)}) copy-start(bf16[1024,1280]{1,0:T(8,128)(2,1)} %reshape.307) | copy-start | bytes 7864324
  270.7 6.8 %copy-start.9 = (bf16[1024,1152]{1,0:T(8,128)(2,1)S(1)}, bf16[1024,1152]{1,0:T(8,128)(2,1)}, u32[]{:S(2)}) copy-start(bf16[1024,1152]{1,0:T(8,128)(2,1)} %reshape.309) | copy-start | bytes 7077892
  277.5 7.0 %copy-start.3 = (f32[1024,1024]{1,0:T(8,128)S(1)}, f32[1024,1024]{1,0:T(8,128)}, u32[]{:S(2)}) copy-start(f32[1024,1024]{1,0:T(8,128)} %copy-done.2) | copy-start | bytes 12582916
  293.7 2.3 copy-start.4
  299.5 7.7 %copy-start.1 = (bf16[2,304,160]{1,2,0:T(8,128)(2,1)S(1)}, bf16[2,304,160]{1,2,0:T(8,128)(2,1)}, u32[]{:S(2)}) copy-start(bf16[2,304,160]{1,2,0:T(8,128)(2,1)} %param.8) | copy-start | bytes 583684
Sparse Core Ops, SparseCore 0:
  31.3 42.5 all-gather.6
  86.0 37.9 all-gather.10
  125.8 39.2 all-gather.12
  167.5 89.7 all-gather.8
